TPU v7x, 32 devices: a whole 2x2x4 slice. The times are simulated.
32 devices in a mesh: seq: 8 (over y, x, core), tp: 4 (over z).
Axes of the slice: x: 2, y: 2, z: 4, core: 2. Of those that a mesh axis runs over, the one named last changes fastest.
Arguments:
- hidden_in: bfloat16 [8192, 2048], P('seq', 'tp'), may hold values from -6 to 6
- segment_ids: int32 [8192], P('seq'), may hold values from 0 to 7, never falling along the last dimension, each value on 1 to 4096 neighbouring positions
- first_gain: float32 [2048], replicated, may hold values from 0.5 to 1.5
- input_weight: bfloat16 [2048, 2816], P(None, 'tp'), may hold values from -0.125 to 0.125
- gelu_weight: bfloat16 [2048, 2816], P(None, 'tp'), may hold values from -0.125 to 0.125
- conv_weight: float32 [4, 2816], P(None, 'tp'), may hold values from -3 to 3
- conv_bias: float32 [2816], P('tp'), may hold values from -3 to 3
- recur_gate: bfloat16 [16, 176, 176], P('tp'), may hold values from -0.4375 to 0.4375
- input_gate: bfloat16 [16, 176, 176], P('tp'), may hold values from -0.4375 to 0.4375
- recur_bias: float32 [2816], P('tp'), may hold values from -4 to 4
- input_bias: float32 [2816], P('tp'), may hold values from -4 to 4
- decay_param: float32 [2816], P('tp'), may hold values from 5 to 15
- output_weight: bfloat16 [2816, 2048], P('tp'), may hold values from -0.3125 to 0.3125
- second_gain: float32 [2048], replicated, may hold values from 0.5 to 1.5
- gate_weight: bfloat16 [2048, 6144], P('seq', 'tp'), may hold values from -0.125 to 0.125
- up_weight: bfloat16 [2048, 6144], P('seq', 'tp'), may hold values from -0.125 to 0.125
- down_weight: bfloat16 [6144, 2048], P('tp', 'seq'), may hold values from -0.109375 to 0.109375
- grad_out: bfloat16 [8192, 2048], P('seq'), may hold values from -6 to 6
Outputs:
- block_out: bfloat16 [8192, 2048], P('seq', 'tp')
- grad_in: bfloat16 [8192, 2048], P('seq', 'tp')
- grad_first_gain: float32 [2048], replicated
- grad_input_weight: float32 [2048, 2816], P(None, 'tp')
- grad_gelu_weight: float32 [2048, 2816], P(None, 'tp')
- grad_conv_weight: float32 [4, 2816], P(None, 'tp')
- grad_conv_bias: float32 [2816], P('tp')
- grad_recur_gate: float32 [16, 176, 176], P('tp')
- grad_input_gate: float32 [16, 176, 176], P('tp')
- grad_recur_bias: float32 [2816], P('tp')
- grad_input_bias: float32 [2816], P('tp')
- grad_decay: float32 [2816], P('tp')
- grad_output_weight: float32 [2816, 2048], P('tp')
- grad_second_gain: float32 [2048], replicated
- grad_gate_weight: float32 [2048, 6144], P('seq', 'tp')
- grad_up_weight: float32 [2048, 6144], P('seq', 'tp')
- grad_down_weight: float32 [6144, 2048], P('tp', 'seq')
- final_states: float32 [8, 2816], P(None, 'tp')
Inputs may be any that keep to these rules, and one draw needn't show every extreme that they name: `segment_ids`: Non-decreasing along the stream; every segment number occurs; each segment has 1 to 4096 tokens and one has exactly 4096.
All inputs are finite; a program needn't handle non-finite values.
Results may differ from a plain program's by a relative error of at most 0.009.
Values may be sent and summed in bfloat16 or wider, within the bound.
No kernel may reach another device: no remote copies, remote signals or barrier semaphores. Data moves between devices by JAX's collectives and lax.ppermute only.
A program may use at most 448 MiB of HBM per device.

v0:
```python
from functools import partial
import jax
import jax.numpy as jnp
from jax import lax
from jax.sharding import PartitionSpec as P

SEGS = 8
EPSILON = 1e-06
DECAY_SCALE = 8.0


def shifted(x, axis, by):
    peers = lax.axis_size(axis)
    pairs = [(i, i + by) for i in range(peers) if 0 <= i + by < peers]
    return lax.ppermute(x, axis, pairs)


def prefix(part, axis, combine, identity, reverse):
    count = lax.axis_size(axis)
    place = lax.axis_index(axis)
    ahead = count - 1 - place if reverse else place
    gathered = jax.tree.map(lambda a: lax.all_gather(a, axis), part)
    state = jax.tree.map(lambda a, e: jnp.zeros_like(a) + jnp.asarray(e, a.dtype), part, identity)

    def one(hop, state):
        source = count - 1 - hop if reverse else hop
        return combine(
            state, jax.tree.map(lambda a: lax.dynamic_index_in_dim(a, source, 0, False), gathered)
        )

    return lax.fori_loop(0, ahead, one, state)


def rms_norm(value, gain):
    return value * lax.rsqrt(jnp.mean(value * value, axis=1, keepdims=True) + EPSILON) * gain


def compose(earlier, later):
    return (earlier[0] * later[0], later[0] * earlier[1] + later[1])


def gate_math(pre_recur, pre_input, conv_val, bias_recur, bias_input, decay_value, restart):
    rate_gate = jax.nn.sigmoid(pre_recur + bias_recur)
    in_gate = jax.nn.sigmoid(pre_input + bias_input)
    log_decay = -DECAY_SCALE * rate_gate * jax.nn.softplus(-decay_value)
    carried = jnp.where(restart, 0.0, jnp.exp(log_decay))
    scaled = jnp.where(restart, 1.0, jnp.sqrt(-jnp.expm1(2.0 * log_decay)))
    return (carried, scaled * in_gate * conv_val)


def contract_first(left, right):
    return lax.dot_general(
        left, right, (((0,), (0,)), ((), ())), preferred_element_type=jnp.float32
    )


def contract_last(left, right):
    return lax.dot_general(
        left, right, (((1,), (1,)), ((), ())), preferred_element_type=jnp.float32
    )


def exact_dot(left, right):
    return jnp.dot(left, right, precision=lax.Precision.HIGHEST, preferred_element_type=jnp.float32)


def exact_first(left, right):
    return lax.dot_general(
        left,
        right,
        (((0,), (0,)), ((), ())),
        precision=lax.Precision.HIGHEST,
        preferred_element_type=jnp.float32,
    )


def on_device(
    hidden_in,
    segment_ids,
    first_gain,
    input_weight,
    gelu_weight,
    conv_weight,
    conv_bias,
    recur_gate,
    input_gate,
    recur_bias,
    input_bias,
    decay_param,
    output_weight,
    second_gain,
    gate_weight,
    up_weight,
    down_weight,
    grad_out,
):
    tok_dev = hidden_in.shape[0]
    share_width = hidden_in.shape[1]
    channels = input_weight.shape[1]
    conv_taps = conv_weight.shape[0]
    halo_rows = conv_taps - 1
    seq_devices = lax.axis_size("seq")
    seq_place = lax.axis_index("seq")
    tp_place = lax.axis_index("tp")
    share_start = tp_place * share_width
    first_device = seq_place == 0
    final_device = seq_place == seq_devices - 1
    ids_float = segment_ids.astype(jnp.float32)
    row_grid = lax.broadcasted_iota(jnp.int32, (tok_dev, tok_dev), 0)
    col_grid = lax.broadcasted_iota(jnp.int32, (tok_dev, tok_dev), 1)
    edge_rows = lax.broadcasted_iota(jnp.int32, (tok_dev, halo_rows), 0)
    edge_cols = lax.broadcasted_iota(jnp.int32, (tok_dev, halo_rows), 1)
    token_place = lax.broadcasted_iota(jnp.int32, (tok_dev, 1), 0)
    full_in = lax.all_gather(hidden_in, "tp", axis=1, tiled=True).astype(jnp.float32)
    normed1, norm1_back = jax.vjp(rms_norm, full_in, first_gain)
    normed1_low = normed1.astype(jnp.bfloat16)
    branch_x = jnp.dot(normed1_low, input_weight, preferred_element_type=jnp.float32)
    branch_y = jnp.dot(normed1_low, gelu_weight, preferred_element_type=jnp.float32)
    prev_rows, prev_ids = shifted(
        (branch_x[tok_dev - halo_rows :], ids_float[tok_dev - halo_rows :]), "seq", 1
    )
    prev_ids = jnp.where(first_device, -1.0, prev_ids)
    ext_ids = jnp.concatenate([prev_ids, ids_float])
    same_list = [
        (ext_ids[halo_rows - offset : halo_rows - offset + tok_dev] == ids_float).astype(
            jnp.float32
        )[:, None]
        for offset in range(conv_taps)
    ]
    lag_list = [
        (col_grid == row_grid - offset).astype(jnp.float32) * same_list[offset]
        for offset in range(conv_taps)
    ]
    edge_list = [
        (edge_cols == edge_rows - offset + halo_rows).astype(jnp.float32) * same_list[offset]
        for offset in range(conv_taps)
    ]
    window_list = [
        exact_dot(lag_list[offset], branch_x) + exact_dot(edge_list[offset], prev_rows)
        for offset in range(conv_taps)
    ]
    conv_out = conv_bias + sum(
        (conv_weight[offset] * window_list[offset] for offset in range(conv_taps))
    )
    blocks_here = recur_gate.shape[0]
    block_size = recur_gate.shape[1]
    conv_low = conv_out.astype(jnp.bfloat16).reshape(tok_dev, blocks_here, block_size)
    pre_recur = jnp.einsum(
        "tbi,bij->tbj", conv_low, recur_gate, preferred_element_type=jnp.float32
    ).reshape(tok_dev, channels)
    pre_input = jnp.einsum(
        "tbi,bij->tbj", conv_low, input_gate, preferred_element_type=jnp.float32
    ).reshape(tok_dev, channels)
    restart = same_list[1] == 0.0
    (carried, drive), gate_back = jax.vjp(
        partial(gate_math, restart=restart),
        pre_recur,
        pre_input,
        conv_out,
        recur_bias,
        input_bias,
        decay_param,
    )
    cum_decay, local_state = lax.associative_scan(compose, (carried, drive), axis=0)
    ones_row = jnp.ones((channels,), jnp.float32)
    zero_row = jnp.zeros((channels,), jnp.float32)
    incoming = prefix(
        (cum_decay[tok_dev - 1], local_state[tok_dev - 1]),
        "seq",
        compose,
        (ones_row, zero_row),
        False,
    )
    state = local_state + cum_decay * incoming[1]
    gelu_y, gelu_y_back = jax.vjp(jax.nn.gelu, branch_y)
    mixed_low = (gelu_y * state).astype(jnp.bfloat16)
    branch_part = jnp.dot(mixed_low, output_weight, preferred_element_type=jnp.float32)
    resid1 = full_in + lax.psum(branch_part, "tp")
    normed2, norm2_back = jax.vjp(rms_norm, resid1, second_gain)
    normed2_low = normed2.astype(jnp.bfloat16)
    resid_share = lax.dynamic_slice_in_dim(resid1, share_start, share_width, 1)
    hidden_cols = gate_weight.shape[1]
    weight_pieces = (
        lax.all_gather(gate_weight, "seq", axis=0, tiled=True),
        lax.all_gather(up_weight, "seq", axis=0, tiled=True),
    )
    columns = normed2_low
    gate_pre = jnp.dot(columns, weight_pieces[0], preferred_element_type=jnp.float32)
    up_pre = jnp.dot(columns, weight_pieces[1], preferred_element_type=jnp.float32)
    activated, act_back = jax.vjp(jax.nn.gelu, gate_pre)
    hid_low = (activated * up_pre).astype(jnp.bfloat16)
    mlp_part = jnp.dot(
        hid_low,
        lax.all_gather(down_weight, "seq", axis=1, tiled=True),
        preferred_element_type=jnp.float32,
    )
    mlp_share = lax.psum_scatter(mlp_part, "tp", scatter_dimension=1, tiled=True)
    block_out = (resid_share + mlp_share).astype(jnp.bfloat16)
    grad_full = grad_out.astype(jnp.float32)
    columns = grad_out
    d_hid = contract_last(columns, lax.all_gather(down_weight, "seq", axis=1, tiled=True))
    d_gate_low = act_back(d_hid * up_pre)[0].astype(jnp.bfloat16)
    d_up_low = (d_hid * activated).astype(jnp.bfloat16)
    weight_pieces = lax.all_gather((gate_weight, up_weight), "seq", axis=0, tiled=True)
    d_norm2_part = contract_last(d_gate_low, weight_pieces[0]) + contract_last(
        d_up_low, weight_pieces[1]
    )
    d_norm2 = lax.psum(d_norm2_part, "tp")
    d_resid_from2, grad_second = norm2_back(d_norm2)
    d_resid1 = grad_full + d_resid_from2
    d_resid_low = d_resid1.astype(jnp.bfloat16)
    d_resid_share = lax.dynamic_slice_in_dim(d_resid1, share_start, share_width, 1)
    mlp_grads = lax.psum_scatter(
        jnp.concatenate(
            [
                contract_first(normed2_low, d_gate_low),
                contract_first(normed2_low, d_up_low),
                contract_first(grad_out, hid_low),
            ],
            axis=1,
        ),
        "seq",
        scatter_dimension=0,
        tiled=True,
    )
    grad_gate_weight = mlp_grads[:, :hidden_cols]
    grad_up_weight = mlp_grads[:, hidden_cols : 2 * hidden_cols]
    grad_down_weight = mlp_grads[:, 2 * hidden_cols :].T
    d_mixed = contract_last(d_resid_low, output_weight)
    grad_out_weight = contract_first(mixed_low, d_resid_low)
    d_state = d_mixed * gelu_y
    d_branch_y = gelu_y_back(d_mixed * state)[0]
    lead_matrix = (col_grid == row_grid + 1).astype(jnp.float32)
    last_mark = (token_place == tok_dev - 1).astype(jnp.float32)
    first_mark = (token_place == 0).astype(jnp.float32)
    coefficient = exact_dot(lead_matrix, carried) + last_mark
    rev_decay, local_grad = lax.associative_scan(
        compose, (coefficient, d_state), reverse=True, axis=0
    )
    outgoing = (carried[0] * rev_decay[0], carried[0] * local_grad[0])
    from_above = prefix(outgoing, "seq", compose, (ones_row, zero_row), True)
    d_state_all = local_grad + rev_decay * from_above[1]
    trail_matrix = (col_grid == row_grid - 1).astype(jnp.float32)
    prev_state = exact_dot(trail_matrix, state) + first_mark * incoming[1]
    d_pre_recur, d_pre_input, d_conv_direct, grad_rbias, grad_ibias, grad_decay = gate_back(
        (d_state_all * prev_state, d_state_all)
    )
    d_recur_low = d_pre_recur.astype(jnp.bfloat16).reshape(tok_dev, blocks_here, block_size)
    d_input_low = d_pre_input.astype(jnp.bfloat16).reshape(tok_dev, blocks_here, block_size)
    grad_recur_gate = jnp.einsum(
        "tbi,tbj->bij", conv_low, d_recur_low, preferred_element_type=jnp.float32
    )
    grad_input_gate = jnp.einsum(
        "tbi,tbj->bij", conv_low, d_input_low, preferred_element_type=jnp.float32
    )
    d_conv_gates = jnp.einsum(
        "tbj,bij->tbi", d_recur_low, recur_gate, preferred_element_type=jnp.float32
    ) + jnp.einsum("tbj,bij->tbi", d_input_low, input_gate, preferred_element_type=jnp.float32)
    d_conv = d_conv_direct + d_conv_gates.reshape(tok_dev, channels)
    grad_conv_bias = jnp.sum(d_conv, axis=0)
    grad_conv_weight = jnp.stack(
        [jnp.sum(d_conv * window_list[offset], axis=0) for offset in range(conv_taps)], axis=0
    )
    tap_grads = [conv_weight[offset] * d_conv for offset in range(conv_taps)]
    d_local = sum((exact_first(lag_list[offset], tap_grads[offset]) for offset in range(conv_taps)))
    d_edge = sum((exact_first(edge_list[offset], tap_grads[offset]) for offset in range(conv_taps)))
    back_rows, next_first = shifted((d_edge, ids_float[:1]), "seq", -1)
    tail_matrix = (edge_rows == tok_dev - halo_rows + edge_cols).astype(jnp.float32)
    d_branch_x = d_local + exact_dot(tail_matrix, back_rows)
    d_x_low = d_branch_x.astype(jnp.bfloat16)
    d_y_low = d_branch_y.astype(jnp.bfloat16)
    grad_in_weight = contract_first(normed1_low, d_x_low)
    grad_gelu_weight = contract_first(normed1_low, d_y_low)
    d_norm1_part = contract_last(d_x_low, input_weight) + contract_last(d_y_low, gelu_weight)
    d_norm1 = lax.psum(d_norm1_part, "tp")
    d_in_from1, grad_first = norm1_back(d_norm1)
    grad_in = (
        d_resid_share + lax.dynamic_slice_in_dim(d_in_from1, share_start, share_width, 1)
    ).astype(jnp.bfloat16)
    next_first = jnp.where(final_device, -1.0, next_first)
    next_ids = jnp.concatenate([ids_float[1:], next_first])
    segment_ends = (next_ids != ids_float).astype(jnp.float32)[:, None]
    member = (segment_ids[:, None] == jnp.arange(SEGS, dtype=jnp.int32)[None, :]).astype(
        jnp.float32
    )
    final_part = lax.dot_general(
        member,
        state * segment_ends,
        (((0,), (0,)), ((), ())),
        precision=lax.Precision.HIGHEST,
        preferred_element_type=jnp.float32,
    )
    summed = lax.psum(
        (
            grad_in_weight,
            grad_gelu_weight,
            grad_out_weight,
            grad_conv_weight,
            grad_conv_bias,
            grad_recur_gate,
            grad_input_gate,
            grad_rbias,
            grad_ibias,
            grad_decay,
            grad_first,
            grad_second,
            final_part,
        ),
        "seq",
    )
    return (
        block_out,
        grad_in,
        summed[10],
        summed[0],
        summed[1],
        summed[3],
        summed[4],
        summed[5],
        summed[6],
        summed[7],
        summed[8],
        summed[9],
        summed[2],
        summed[11],
        grad_gate_weight,
        grad_up_weight,
        grad_down_weight,
        summed[12],
    )


def solution(mesh):
    return jax.shard_map(
        on_device,
        mesh=mesh,
        in_specs=(
            P("seq", "tp"),
            P("seq"),
            P(),
            P(None, "tp"),
            P(None, "tp"),
            P(None, "tp"),
            P("tp"),
            P("tp", None, None),
            P("tp", None, None),
            P("tp"),
            P("tp"),
            P("tp"),
            P("tp", None),
            P(),
            P("seq", "tp"),
            P("seq", "tp"),
            P("tp", "seq"),
            P("seq", None),
        ),
        out_specs=(
            P("seq", "tp"),
            P("seq", "tp"),
            P(),
            P(None, "tp"),
            P(None, "tp"),
            P(None, "tp"),
            P("tp"),
            P("tp", None, None),
            P("tp", None, None),
            P("tp"),
            P("tp"),
            P("tp"),
            P("tp", None),
            P(),
            P("seq", "tp"),
            P("seq", "tp"),
            P("tp", "seq"),
            P(None, "tp"),
        ),
        check_vma=False,
    )
```

profile of v0, /device:TPU:0, one launch (start us, length us, event | category | flops | bytes accessed | tf_op | source)
XLA Modules:
  0.0 4483.2 jit_solution(468092202798711800)
XLA Ops:
  20.0 73.9 %all-gather.9.cloned.1.call-done = bf16[1024,2048]{1,0:T(8,128)(2,1)} async-done(((bf16[1024,512]{1,0:T(8,128)(2,1)}), bf16[1024,2048]{1,0:T(8,128)(2,1)}) %all-gather.9.cloned.1.call-update) | async-done | bytes 4194320 | tf_op jit(solution)/shard_map/all_gather | solution.py:114
  166.0 51.2 %slice.745 = f32[511,704]{0,1:T(8,128)} slice(f32[1024,704]{0,1:T(8,128)} %copy-done.17), slice={[2:1024:2], [0:704:1]} | slice | bytes 2877952 | tf_op jit(solution)/shard_map/slice | solution.py:164
  217.2 51.3 %slice.675 = f32[512,704]{0,1:T(8,128)} slice(f32[1024,704]{0,1:T(8,128)} %copy-done.17), slice={[1:1024:2], [0:704:1]} | slice | bytes 2883584 | tf_op jit(solution)/shard_map/slice | solution.py:164
  268.5 51.2 %slice.674 = f32[512,704]{0,1:T(8,128)} slice(f32[1024,704]{0,1:T(8,128)} %copy-done.17), slice={[0:1023:2], [0:704:1]} | slice | bytes 2883584 | tf_op jit(solution)/shard_map/slice | solution.py:164
  323.6 51.6 %slice.677 = f32[512,704]{0,1:T(8,128)} slice(f32[1024,704]{0,1:T(8,128)} %copy-done.16), slice={[0:1023:2], [0:704:1]} | slice | bytes 2883584 | tf_op jit(solution)/shard_map/slice | solution.py:164
  375.2 51.3 %slice.673 = f32[512,704]{0,1:T(8,128)} slice(f32[1024,704]{0,1:T(8,128)} %copy-done.16), slice={[1:1024:2], [0:704:1]} | slice | bytes 2883584 | tf_op jit(solution)/shard_map/slice | solution.py:164
  432.9 28.2 slice.743
  461.1 28.5 slice.681
  489.6 28.3 slice.680
  519.6 28.3 slice.683
  547.9 28.3 slice.679
  576.3 28.4 slice.678
  884.9 51.3 %slice.672 = f32[511,704]{0,1:T(8,128)} slice(f32[1024,704]{0,1:T(8,128)} %copy-done.16), slice={[2:1024:2], [0:704:1]} | slice | bytes 2877952 | tf_op jit(solution)/shard_map/slice | solution.py:164
  1169.7 28.8 pad.280
  1198.5 28.7 pad.260
  1227.2 28.7 pad.261
  1255.9 28.9 pad.281
  1288.0 57.1 %pad.283 = f32[1024,704]{0,1:T(8,128)} pad(f32[512,704]{0,1:T(8,128)} %add.730, f32[]{:T(128)} %constant.114.clone.1), padding=1_0_1x0_0_0 | pad | bytes 4325380 | tf_op jit(solution)/shard_map/pad | solution.py:164
  1354.5 57.2 %pad.282 = f32[1024,704]{0,1:T(8,128)} pad(f32[512,704]{0,1:T(8,128)} %pad_maximum_fusion.2, f32[]{:T(128)} %constant.114.clone.1), padding=0_1_1x0_0_0 | pad | bytes 4325380 | tf_op jit(solution)/shard_map/pad | solution.py:164
  1422.4 57.1 %pad.263 = f32[1024,704]{0,1:T(8,128)} pad(f32[512,704]{0,1:T(8,128)} %add.719, f32[]{:T(128)} %constant.114.clone.1), padding=1_0_1x0_0_0 | pad | bytes 4325380 | tf_op jit(solution)/shard_map/pad | solution.py:164
  1482.4 57.1 %pad.262 = f32[1024,704]{0,1:T(8,128)} pad(f32[512,704]{0,1:T(8,128)} %pad_maximum_fusion.1, f32[]{:T(128)} %constant.114.clone.1), padding=0_1_1x0_0_0 | pad | bytes 4325380 | tf_op jit(solution)/shard_map/pad | solution.py:164
  1569.9 287.2 %all-reduce.87.cloned.1.call-done = f32[1024,2048]{1,0:T(8,128)} async-done(((f32[1024,2048]{1,0:T(8,128)}), f32[1024,2048]{1,0:T(8,128)}) %all-reduce.87.cloned.1.call-update) | async-done | bytes 8388624 | tf_op jit(solution)/shard_map/psum | solution.py:178
  1940.5 51.5 %slice.777 = f32[512,704]{0,1:T(8,128)} slice(f32[1024,704]{0,1:T(8,128)} %copy-done.46), slice={[1:1024:2], [0:704:1]} | slice | bytes 2883584 | tf_op jit(solution)/shard_map/slice | solution.py:237
  1991.9 51.2 %slice.770 = f32[512,704]{0,1:T(8,128)} slice(f32[1024,704]{0,1:T(8,128)} %copy-done.46), slice={[0:1023:2], [0:704:1]} | slice | bytes 2883584 | tf_op jit(solution)/shard_map/slice | solution.py:237
  2043.2 51.3 %slice.768 = f32[511,704]{0,1:T(8,128)} slice(f32[1024,704]{0,1:T(8,128)} %copy-done.46), slice={[1:1022:2], [0:704:1]} | slice | bytes 2877952 | tf_op jit(solution)/shard_map/slice | solution.py:237
  2146.3 74.1 %all-reduce.89.cloned.1.call-done = f32[1024,2048]{1,0:T(8,128)} async-done(((f32[1024,2048]{1,0:T(8,128)}), f32[1024,2048]{1,0:T(8,128)}) %all-reduce.89.cloned.1.call-update) | async-done | bytes 8388624 | tf_op jit(solution)/shard_map/psum | solution.py:208
  2247.3 51.3 %slice.774 = f32[512,704]{0,1:T(8,128)} slice(f32[1024,704]{0,1:T(8,128)} %get-tuple-element.297), slice={[0:1023:2], [0:704:1]} | slice | bytes 2883584 | tf_op jit(solution)/shard_map/slice | solution.py:237
  2298.6 51.3 %slice.772 = f32[512,704]{0,1:T(8,128)} slice(f32[1024,704]{0,1:T(8,128)} %get-tuple-element.297), slice={[1:1024:2], [0:704:1]} | slice | bytes 2883584 | tf_op jit(solution)/shard_map/slice | solution.py:237
  2381.3 28.7 slice.782
  2410.0 28.3 slice.781
  2438.3 28.3 slice.784
  2466.6 28.3 slice.780
  2682.4 51.3 %slice.846 = f32[511,704]{0,1:T(8,128)} slice(f32[1024,704]{0,1:T(8,128)} %get-tuple-element.297), slice={[1:1022:2], [0:704:1]} | slice | bytes 2877952 | tf_op jit(solution)/shard_map/slice | solution.py:237
  2737.2 28.2 slice.844
  2765.4 28.2 slice.779
  3155.2 28.6 pad.320
  3186.1 28.7 pad.300
  3214.8 29.0 pad.301
  3243.7 28.7 pad.321
  3282.7 57.1 %pad.302 = f32[1024,704]{0,1:T(8,128)} pad(f32[512,704]{0,1:T(8,128)} %pad_maximum_fusion.3, f32[]{:T(128)} %constant.114.clone.1), padding=0_1_1x0_0_0 | pad | bytes 4325380 | tf_op jit(solution)/shard_map/pad | solution.py:237
  3339.8 57.2 %pad.303 = f32[1024,704]{0,1:T(8,128)} pad(f32[512,704]{0,1:T(8,128)} %add.769, f32[]{:T(128)} %constant.114.clone.1), padding=1_0_1x0_0_0 | pad | bytes 4325380 | tf_op jit(solution)/shard_map/pad | solution.py:237
  3402.1 25.7 rev.8
  3430.7 57.1 %pad.322 = f32[1024,704]{0,1:T(8,128)} pad(f32[512,704]{0,1:T(8,128)} %pad_maximum_fusion.4, f32[]{:T(128)} %constant.114.clone.1), padding=0_1_1x0_0_0 | pad | bytes 4325380 | tf_op jit(solution)/shard_map/pad | solution.py:237
  3487.8 57.3 %pad.323 = f32[1024,704]{0,1:T(8,128)} pad(f32[512,704]{0,1:T(8,128)} %add.780, f32[]{:T(128)} %constant.114.clone.1), padding=1_0_1x0_0_0 | pad | bytes 4325380 | tf_op jit(solution)/shard_map/pad | solution.py:237
  3550.2 25.7 rev.9
  3789.2 197.0 %all-reduce.91.cloned.1.call-done = f32[1024,2048]{1,0:T(8,128)} async-done(((f32[1024,2048]{1,0:T(8,128)}), f32[1024,2048]{1,0:T(8,128)}) %all-reduce.91.cloned.1.call-update) | async-done | bytes 8388624 | tf_op jit(solution)/shard_map/psum | solution.py:275
  4025.6 188.5 %reduce-scatter.5.cloned.1.call-done = f32[256,4608]{0,1:T(8,128)} async-done(((f32[2048,4608]{0,1:T(8,128)}), f32[256,4608]{0,1:T(8,128)}) %reduce-scatter.5.cloned.1.call-update) | async-done | bytes 4718608 | tf_op jit(solution)/shard_map/reduce_scatter | solution.py:213
  4224.8 236.9 %all-reduce.93.cloned.1.call-done = (f32[2048,704]{0,1:T(8,128)}, f32[2048,704]{0,1:T(8,128)}, f32[4,176,176]{2,1,0:T(8,128)}, f32[4,176,176]{2,1,0:T(8,128)}, f32[704,2048]{1,0:T(8,128)}) async-done(((f32[2048,704]{0,1:T(8,128)}, f32[2048,704]{0,1:T(8,128)}, f32[4,176,176]{2,1,0:T(8,128)}, f32[4,176,176]{2,1,0:T(8,128)}, f32[704,2048]{1,0:T(8,128)}), (f32[2048,704]{0,1:T(8,128)}, f32[2048,704]{0,1:T(8,128)}, ...) | async-done | bytes 18292752 | tf_op jit(solution)/shard_map/psum | solution.py:293
  (787 shorter events, 1712.4 us)
Async XLA Ops:
  8.0 1542.1 %copy-start = (bf16[2048,704]{0,1:T(8,128)(2,1)S(1)}, bf16[2048,704]{0,1:T(8,128)(2,1)}, u32[]{:S(2)}) copy-start(bf16[2048,704]{0,1:T(8,128)(2,1)} %param.26) | copy-start | bytes 8650756
  8.0 89.7 %copy-start.137 = (f32[2048]{0:T(1024)S(1)}, f32[2048]{0:T(1024)}, u32[]{:S(2)}) copy-start(f32[2048]{0:T(1024)} %param.24) | copy-start | bytes 24580
  8.0 85.9 %all-gather.9.cloned.1.call-start = ((), (), s32[]{:S(2)}) async-start(), calls=%async_computation.2 | async-start | bytes 5242880 | tf_op jit(solution)/shard_map/all_gather | solution.py:114
  8.8 1848.3 %all-reduce.87.cloned.1.call-start = ((), (), s32[]{:S(2)}) async-start(), calls=%async_computation.3 | async-start | bytes 16777216 | tf_op jit(solution)/shard_map/psum | solution.py:178
  9.7 10.2 collective-permute-start
  12.5 5.4 collective-permute-start.3
  13.9 110.8 %copy-start.143 = (s32[1024]{0:T(1024)}, s32[1024]{0:T(1024)S(1)}, u32[]{:S(2)}) copy-start(s32[1024]{0:T(1024)S(1)} %iota_add_fusion.4) | copy-start | bytes 12292
  13.9 130.4 %copy-start.114 = (s32[1024]{0:T(1024)}, s32[1024]{0:T(1024)S(1)}, u32[]{:S(2)}) copy-start(s32[1024]{0:T(1024)S(1)} %iota_add_fusion.1) | copy-start | bytes 12292
  13.9 135.7 %copy-start.112 = (s32[1024]{0:T(1024)}, s32[1024]{0:T(1024)S(1)}, u32[]{:S(2)}) copy-start(s32[1024]{0:T(1024)S(1)} %iota_add_fusion.5) | copy-start | bytes 12292
  13.9 133.0 %copy-start.116 = (s32[1024]{0:T(1024)}, s32[1024]{0:T(1024)S(1)}, u32[]{:S(2)}) copy-start(s32[1024]{0:T(1024)S(1)} %iota_add_fusion.3) | copy-start | bytes 12292
  14.0 100.8 %copy-start.145 = (s32[1024]{0:T(1024)}, s32[1024]{0:T(1024)S(1)}, u32[]{:S(2)}) copy-start(s32[1024]{0:T(1024)S(1)} %iota_add_fusion.2) | copy-start | bytes 12292
  14.0 91.0 %copy-start.147 = (s32[1024]{0:T(1024)}, s32[1024]{0:T(1024)S(1)}, u32[]{:S(2)}) copy-start(s32[1024]{0:T(1024)S(1)} %iota_add_fusion) | copy-start | bytes 12292
  14.9 137.5 %copy-start.104 = (f32[704]{0:T(1024)}, f32[704]{0:T(1024)S(1)}, u32[]{:S(2)}) copy-start(f32[704]{0:T(1024)S(1)} %get-tuple-element.233) | copy-start | bytes 8452
  14.9 137.5 %copy-start.106 = (f32[704]{0:T(1024)}, f32[704]{0:T(1024)S(1)}, u32[]{:S(2)}) copy-start(f32[704]{0:T(1024)S(1)} %get-tuple-element.234) | copy-start | bytes 8452
  14.9 137.5 %copy-start.108 = (f32[704]{0:T(1024)}, f32[704]{0:T(1024)S(1)}, u32[]{:S(2)}) copy-start(f32[704]{0:T(1024)S(1)} %get-tuple-element.236) | copy-start | bytes 8452
  14.9 137.5 %copy-start.110 = (f32[704]{0:T(1024)}, f32[704]{0:T(1024)S(1)}, u32[]{:S(2)}) copy-start(f32[704]{0:T(1024)S(1)} %get-tuple-element.235) | copy-start | bytes 8452
  16.2 303.5 %copy-start.101 = (f32[704]{0:T(1024)}, f32[704]{0:T(1024)S(1)}, u32[]{:S(2)}) copy-start(f32[704]{0:T(1024)S(1)} %get-tuple-element.390) | copy-start | bytes 8452
  19.9 129.8 %copy-start.118 = (f32[1024]{0:T(1024)}, f32[1024]{0:T(1024)S(1)}, u32[]{:S(2)}) copy-start(f32[1024]{0:T(1024)S(1)} %get-tuple-element.388) | copy-start | bytes 12292
  20.0 124.3 %copy-start.122 = (f32[1024]{0:T(1024)}, f32[1024]{0:T(1024)S(1)}, u32[]{:S(2)}) copy-start(f32[1024]{0:T(1024)S(1)} %get-tuple-element.386) | copy-start | bytes 12292
  20.0 127.0 %copy-start.120 = (f32[1024]{0:T(1024)}, f32[1024]{0:T(1024)S(1)}, u32[]{:S(2)}) copy-start(f32[1024]{0:T(1024)S(1)} %get-tuple-element.285) | copy-start | bytes 12292
  20.0 132.4 %copy-start.124 = (f32[1024]{0:T(1024)}, f32[1024]{0:T(1024)S(1)}, u32[]{:S(2)}) copy-start(f32[1024]{0:T(1024)S(1)} %get-tuple-element.385) | copy-start | bytes 12292
  20.0 299.7 %copy-start.132 = (pred[1024]{0:T(1024)(128)(4,1)}, pred[1024]{0:T(1024)(128)(4,1)S(1)}, u32[]{:S(2)}) copy-start(pred[1024]{0:T(1024)(128)(4,1)S(1)} %get-tuple-element.284) | copy-start | bytes 3076
  97.8 1452.3 %copy-start.129 = (f32[1024]{0:T(1024)}, f32[1024]{0:T(1024)S(1)}, u32[]{:S(2)}) copy-start(f32[1024]{0:T(1024)S(1)} %fusion.172) | copy-start | bytes 12292
  103.0 41.3 collective-permute-start.1
  714.5 47.9 %copy-start.32 = (f32[128,704]{0,1:T(8,128)}, f32[128,704]{0,1:T(8,128)S(1)}, u32[]{:S(2)}) copy-start(f32[128,704]{0,1:T(8,128)S(1)} %get-tuple-element.384) | copy-start | bytes 1081348
  762.3 22.0 copy-start.35
  884.9 51.3 %copy-start.44 = (f32[16,704]{0,1:T(8,128)S(1)}, f32[16,704]{0,1:T(8,128)}, u32[]{:S(2)}) copy-start(f32[16,704]{0,1:T(8,128)} %get-tuple-element.377) | copy-start | bytes 135172
  1057.2 29.8 copy-start.33
  1102.6 45.4 %copy-start.89 = (f32[128,704]{0,1:T(8,128)S(1)}, f32[128,704]{0,1:T(8,128)}, u32[]{:S(2)}) copy-start(f32[128,704]{0,1:T(8,128)} %add.728) | copy-start | bytes 1081348
  1411.7 67.8 %copy-start.80 = (f32[1,704]{0,1:T(8,128)S(1)}, f32[1,704]{0,1:T(8,128)}, u32[]{:S(2)}) copy-start(f32[1,704]{0,1:T(8,128)} %slice.879) | copy-start | bytes 8452
  1568.1 300.9 %all-gather.13.cloned.1.call-start = ((), (), s32[]{:S(2)}) async-start(), calls=%async_computation.5 | async-start | bytes 7077888 | tf_op jit(solution)/shard_map/all_gather | solution.py:185
  1568.7 312.3 %all-gather.11.cloned.1.call-start = ((), (), s32[]{:S(2)}) async-start(), calls=%async_computation.4 | async-start | bytes 7077888 | tf_op jit(solution)/shard_map/all_gather | solution.py:184
  1569.3 323.5 %all-gather.15.cloned.1.call-start = ((), (), s32[]{:S(2)}) async-start(), calls=%async_computation.6 | async-start | bytes 7077888 | tf_op jit(solution)/shard_map/all_gather | solution.py:194
  1569.8 296.4 %copy-start.103 = (f32[2048]{0:T(1024)S(1)}, f32[2048]{0:T(1024)}, u32[]{:S(2)}) copy-start(f32[2048]{0:T(1024)} %param.35) | copy-start | bytes 24580
  1569.8 650.6 %all-reduce.89.cloned.1.call-start = ((), (), s32[]{:S(2)}) async-start(), calls=%async_computation.8 | async-start | bytes 16777216 | tf_op jit(solution)/shard_map/psum | solution.py:208
  1930.5 1855.1 %reduce-scatter.3.cloned.1.call-start = ((), (), s32[]{:S(2)}) async-start(), calls=%async_computation.7 | async-start | bytes 10485760 | tf_op jit(solution)/shard_map/reduce_scatter | solution.py:197
  2146.3 1839.9 %all-reduce.91.cloned.1.call-start = ((), (), s32[]{:S(2)}) async-start(), calls=%async_computation.9 | async-start | bytes 16777216 | tf_op jit(solution)/shard_map/psum | solution.py:275
  3088.0 46.5 %copy-start.90 = (f32[128,704]{0,1:T(8,128)S(1)}, f32[128,704]{0,1:T(8,128)}, u32[]{:S(2)}) copy-start(f32[128,704]{0,1:T(8,128)} %add.778) | copy-start | bytes 1081348
  3154.1 29.8 copy-start.84
  3402.1 25.7 copy-start.79
  3550.2 46.8 %copy-start.102 = (f32[704]{0:T(1024)S(1)}, f32[704]{0:T(1024)}, u32[]{:S(2)}) copy-start(f32[704]{0:T(1024)} %copy-done.101) | copy-start | bytes 8452
  3550.2 46.8 %copy-start.133 = (pred[1024]{0:T(1024)(128)(4,1)S(1)}, pred[1024]{0:T(1024)(128)(4,1)}, u32[]{:S(2)}) copy-start(pred[1024]{0:T(1024)(128)(4,1)} %copy-done.132) | copy-start | bytes 3076
  3642.6 42.3 collective-permute-start.2
  3696.2 517.9 %reduce-scatter.5.cloned.1.call-start = ((), (), s32[]{:S(2)}) async-start(), calls=%async_computation.10 | async-start | bytes 42467328 | tf_op jit(solution)/shard_map/reduce_scatter | solution.py:213
  3752.8 708.9 %all-reduce.93.cloned.1.call-start = ((), (), s32[]{:S(2)}) async-start(), calls=%async_computation.11 | async-start | bytes 37486592 | tf_op jit(solution)/shard_map/psum | solution.py:293
  3789.2 205.3 %copy-start.131 = (f32[2048]{0:T(1024)S(1)}, f32[2048]{0:T(1024)}, u32[]{:S(2)}) copy-start(f32[2048]{0:T(1024)} %get-tuple-element.220) | copy-start | bytes 24580
  3789.2 205.3 %copy-start.134 = (f32[704]{0:T(1024)S(1)}, f32[704]{0:T(1024)}, u32[]{:S(2)}) copy-start(f32[704]{0:T(1024)} %get-tuple-element.270) | copy-start | bytes 8452
  3789.2 230.8 %copy-start.127 = (f32[1024]{0:T(1024)S(1)}, f32[1024]{0:T(1024)}, u32[]{:S(2)}) copy-start(f32[1024]{0:T(1024)} %copy-done.126) | copy-start | bytes 12292
  (130 other events, 752.8 us)
Sparse Core Ops, SparseCore 0:
  10.5 83.4 all-gather.8
  1568.2 288.8 all-reduce.86
  1930.6 289.8 all-reduce.88
  2222.7 143.4 reduce-scatter.2
  3696.3 289.8 all-reduce.90
  3989.7 224.3 reduce-scatter.4
  4220.6 241.0 all-reduce.92
Sparse Core Ops, SparseCore 1:
  1570.4 43.4 all-gather.12
  1615.6 45.3 all-gather.10
  1662.8 46.5 all-gather.14
where the time goes:
time: 4510 us; the launch traced here: 4480 us
  local copies, waits for them, and re-layouts  2710 us (60%)
  waiting for transfers between devices  1060 us (24%)
  other arithmetic  323 us (7%)
  matrix products  302 us (7%)
  blocking collectives  61.7 us (1%)
    slice x63, local copies, waits for them, and re-layouts, on_device(): lax.associative_scan(compose, (coefficient, d_state), reverse=True, axis=0)  809 us
    slice x59, local copies, waits for them, and re-layouts, on_device(): lax.associative_scan(compose, (carried, drive), axis=0)  741 us
    pad x36, local copies, waits for them, and re-layouts, on_device(): lax.associative_scan(compose, (coefficient, d_state), reverse=True, axis=0)  508 us
    pad x36, local copies, waits for them, and re-layouts, on_device(): lax.associative_scan(compose, (carried, drive), axis=0)  500 us
    psum x1, waiting for transfers between devices, on_device(): resid1 = full_in + lax.psum(branch_part, 'tp')  287 us
    psum x1, waiting for transfers between devices, on_device(): lax.psum((grad_in_weight, grad_gelu_weight, grad_out_weight, grad_conv_we...  237 us
    psum x1, waiting for transfers between devices, on_device(): d_norm1 = lax.psum(d_norm1_part, 'tp')  197 us
    reduce_scatter x1, waiting for transfers between devices, on_device(): lax.psum_scatter(jnp.concatenate([contract_first(normed2_low, d_gate_low)...  189 us
  transfers between devices with their start and end apart: 14, of which 7 were waited for; matrix products, arithmetic and copies ran while one was open for 41% of the time, Pallas kernels for 0%

commit v1 on v0

--- a/solution.py
+++ b/solution.py
@@ -7,6 +7,12 @@
 SEGS = 8
 EPSILON = 1e-06
 DECAY_SCALE = 8.0
+
+
+def gather_and_add(x, axis):
+    shards = lax.all_gather(x, axis, axis=0, tiled=False)
+    total = shards.sum(axis=0)
+    return total
 
 
 def shifted(x, axis, by):
@@ -175,7 +181,7 @@
     gelu_y, gelu_y_back = jax.vjp(jax.nn.gelu, branch_y)
     mixed_low = (gelu_y * state).astype(jnp.bfloat16)
     branch_part = jnp.dot(mixed_low, output_weight, preferred_element_type=jnp.float32)
-    resid1 = full_in + lax.psum(branch_part, "tp")
+    resid1 = full_in + gather_and_add(branch_part, "tp")
     normed2, norm2_back = jax.vjp(rms_norm, resid1, second_gain)
     normed2_low = normed2.astype(jnp.bfloat16)
     resid_share = lax.dynamic_slice_in_dim(resid1, share_start, share_width, 1)

time: 4510 us -> 4890 us (1.084)
  waiting for transfers between devices: 1060 us -> 1420 us
    all_gather x0 -> x1, waiting for transfers between devices: none -> 558 us  [gather_and_add(): shards = lax.all_gather(x, axis, axis=0, tiled=False)]
    psum x1 -> x0, waiting for transfers between devices: 287 us -> none  [on_device(): resid1 = full_in + lax.psum(branch_part, 'tp')]
  transfers between devices with their start and end apart: 14 -> 14, of which waited for: 7 -> 10; matrix products, arithmetic and copies ran while one was open for 41% -> 39% of each run, Pallas kernels for 0% -> 0%
where the time goes in v1:
time: 4890 us; the launch traced here: 4870 us
  local copies, waits for them, and re-layouts  2710 us (55%)
  waiting for transfers between devices  1420 us (29%)
  other arithmetic  343 us (7%)
  matrix products  305 us (6%)
  blocking collectives  61.7 us (1%)
    slice x63, local copies, waits for them, and re-layouts, on_device(): lax.associative_scan(compose, (coefficient, d_state), reverse=True, axis=0)  809 us
    slice x59, local copies, waits for them, and re-layouts, on_device(): lax.associative_scan(compose, (carried, drive), axis=0)  741 us
    all_gather x1, waiting for transfers between devices, gather_and_add(): shards = lax.all_gather(x, axis, axis=0, tiled=False)  558 us
    pad x36, local copies, waits for them, and re-layouts, on_device(): lax.associative_scan(compose, (coefficient, d_state), reverse=True, axis=0)  508 us
    pad x36, local copies, waits for them, and re-layouts, on_device(): lax.associative_scan(compose, (carried, drive), axis=0)  506 us
    psum x1, waiting for transfers between devices, on_device(): lax.psum((grad_in_weight, grad_gelu_weight, grad_out_weight, grad_conv_we...  237 us
    psum x1, waiting for transfers between devices, on_device(): d_norm1 = lax.psum(d_norm1_part, 'tp')  197 us
    reduce_scatter x1, waiting for transfers between devices, on_device(): lax.psum_scatter(jnp.concatenate([contract_first(normed2_low, d_gate_low)...  189 us
  transfers between devices with their start and end apart: 14, of which 10 were waited for; matrix products, arithmetic and copies ran while one was open for 39% of the time, Pallas kernels for 0%

profile of v1, /device:TPU:0, one launch (start us, length us, event | category | flops | bytes accessed | tf_op | source)
XLA Modules:
  0.0 4865.3 jit_solution(5706910985519011430)
XLA Ops:
  19.1 74.0 %all-gather.11.cloned.1.call-done = bf16[1024,2048]{1,0:T(8,128)(2,1)} async-done(((bf16[1024,512]{1,0:T(8,128)(2,1)}), bf16[1024,2048]{1,0:T(8,128)(2,1)}) %all-gather.11.cloned.1.call-update) | async-done | bytes 4194320 | tf_op jit(solution)/shard_map/all_gather | solution.py:120
  163.2 51.3 %slice.675 = f32[512,704]{0,1:T(8,128)} slice(f32[1024,704]{0,1:T(8,128)} %get-tuple-element.281), slice={[1:1024:2], [0:704:1]} | slice | bytes 2883584 | tf_op jit(solution)/shard_map/slice | solution.py:170
  214.5 51.2 %slice.674 = f32[512,704]{0,1:T(8,128)} slice(f32[1024,704]{0,1:T(8,128)} %get-tuple-element.281), slice={[0:1023:2], [0:704:1]} | slice | bytes 2883584 | tf_op jit(solution)/shard_map/slice | solution.py:170
  269.6 51.3 %slice.673 = f32[512,704]{0,1:T(8,128)} slice(f32[1024,704]{0,1:T(8,128)} %exponential_select_fusion), slice={[1:1024:2], [0:704:1]} | slice | bytes 2883584 | tf_op jit(solution)/shard_map/slice | solution.py:170
  320.9 51.6 %slice.677 = f32[512,704]{0,1:T(8,128)} slice(f32[1024,704]{0,1:T(8,128)} %exponential_select_fusion), slice={[0:1023:2], [0:704:1]} | slice | bytes 2883584 | tf_op jit(solution)/shard_map/slice | solution.py:170
  377.5 28.2 slice.743
  405.7 28.3 slice.681
  434.1 28.4 slice.678
  462.4 28.3 slice.679
  490.8 28.3 slice.680
  519.1 28.3 slice.683
  827.7 51.2 %slice.745 = f32[511,704]{0,1:T(8,128)} slice(f32[1024,704]{0,1:T(8,128)} %get-tuple-element.281), slice={[2:1024:2], [0:704:1]} | slice | bytes 2877952 | tf_op jit(solution)/shard_map/slice | solution.py:170
  878.9 51.2 %slice.672 = f32[511,704]{0,1:T(8,128)} slice(f32[1024,704]{0,1:T(8,128)} %exponential_select_fusion), slice={[2:1024:2], [0:704:1]} | slice | bytes 2877952 | tf_op jit(solution)/shard_map/slice | solution.py:170
  1170.5 28.8 pad.280
  1199.3 28.7 pad.281
  1231.2 57.1 %pad.283 = f32[1024,704]{0,1:T(8,128)} pad(f32[512,704]{0,1:T(8,128)} %add.728, f32[]{:T(128)} %constant.114.clone.1), padding=1_0_1x0_0_0 | pad | bytes 4325380 | tf_op jit(solution)/shard_map/pad | solution.py:170
  1288.3 28.7 pad.261
  1319.2 28.7 pad.260
  1357.3 57.2 %pad.282 = f32[1024,704]{0,1:T(8,128)} pad(f32[512,704]{0,1:T(8,128)} %pad_maximum_fusion.2, f32[]{:T(128)} %constant.114.clone.1), padding=0_1_1x0_0_0 | pad | bytes 4325380 | tf_op jit(solution)/shard_map/pad | solution.py:170
  1425.2 57.1 %pad.263 = f32[1024,704]{0,1:T(8,128)} pad(f32[512,704]{0,1:T(8,128)} %add.717, f32[]{:T(128)} %constant.114.clone.1), padding=1_0_1x0_0_0 | pad | bytes 4325380 | tf_op jit(solution)/shard_map/pad | solution.py:170
  1485.2 57.1 %pad.262 = f32[1024,704]{0,1:T(8,128)} pad(f32[512,704]{0,1:T(8,128)} %pad_maximum_fusion.1, f32[]{:T(128)} %constant.114.clone.1), padding=0_1_1x0_0_0 | pad | bytes 4325380 | tf_op jit(solution)/shard_map/pad | solution.py:170
  1572.9 557.7 %all-gather.19.cloned.1.call-done = f32[4096,2048]{1,0:T(8,128)} async-done(((f32[1024,2048]{1,0:T(8,128)}), f32[4096,2048]{1,0:T(8,128)}) %all-gather.19.cloned.1.call-update) | async-done | bytes 33554448 | tf_op jit(solution)/shard_map/all_gather | solution.py:13
  2188.0 35.6 all-gather.15.cloned.1.call-done
  2235.3 36.7 all-gather.17.cloned.1.call-done
  2320.4 51.4 %slice.770 = f32[512,704]{0,1:T(8,128)} slice(f32[1024,704]{0,1:T(8,128)} %fusion.89), slice={[0:1023:2], [0:704:1]} | slice | bytes 2883584 | tf_op jit(solution)/shard_map/slice | solution.py:243
  2371.8 51.3 %slice.777 = f32[512,704]{0,1:T(8,128)} slice(f32[1024,704]{0,1:T(8,128)} %fusion.89), slice={[1:1024:2], [0:704:1]} | slice | bytes 2883584 | tf_op jit(solution)/shard_map/slice | solution.py:243
  2423.2 51.3 %slice.768 = f32[511,704]{0,1:T(8,128)} slice(f32[1024,704]{0,1:T(8,128)} %fusion.89), slice={[1:1022:2], [0:704:1]} | slice | bytes 2877952 | tf_op jit(solution)/shard_map/slice | solution.py:243
  2528.3 74.1 %all-reduce.86.cloned.1.call-done = f32[1024,2048]{1,0:T(8,128)} async-done(((f32[1024,2048]{1,0:T(8,128)}), f32[1024,2048]{1,0:T(8,128)}) %all-reduce.86.cloned.1.call-update) | async-done | bytes 8388624 | tf_op jit(solution)/shard_map/psum | solution.py:214
  2629.2 51.3 %slice.774 = f32[512,704]{0,1:T(8,128)} slice(f32[1024,704]{0,1:T(8,128)} %get-tuple-element.297), slice={[0:1023:2], [0:704:1]} | slice | bytes 2883584 | tf_op jit(solution)/shard_map/slice | solution.py:243
  2680.5 51.3 %slice.772 = f32[512,704]{0,1:T(8,128)} slice(f32[1024,704]{0,1:T(8,128)} %get-tuple-element.297), slice={[1:1024:2], [0:704:1]} | slice | bytes 2883584 | tf_op jit(solution)/shard_map/slice | solution.py:243
  2763.2 28.7 slice.782
  2791.9 28.3 slice.781
  2820.2 28.3 slice.780
  2848.6 28.3 slice.784
  3160.4 28.2 slice.844
  3188.7 28.2 slice.779
  3222.1 51.5 %slice.846 = f32[511,704]{0,1:T(8,128)} slice(f32[1024,704]{0,1:T(8,128)} %get-tuple-element.297), slice={[1:1022:2], [0:704:1]} | slice | bytes 2877952 | tf_op jit(solution)/shard_map/slice | solution.py:243
  3499.6 28.7 pad.321
  3566.1 28.8 pad.320
  3594.9 28.7 pad.301
  3625.9 28.7 pad.300
  3664.9 57.3 %pad.302 = f32[1024,704]{0,1:T(8,128)} pad(f32[512,704]{0,1:T(8,128)} %pad_maximum_fusion.3, f32[]{:T(128)} %constant.114.clone.1), padding=0_1_1x0_0_0 | pad | bytes 4325380 | tf_op jit(solution)/shard_map/pad | solution.py:243
  3722.2 57.3 %pad.303 = f32[1024,704]{0,1:T(8,128)} pad(f32[512,704]{0,1:T(8,128)} %add.767, f32[]{:T(128)} %constant.114.clone.1), padding=1_0_1x0_0_0 | pad | bytes 4325380 | tf_op jit(solution)/shard_map/pad | solution.py:243
  3813.5 57.5 %pad.322 = f32[1024,704]{0,1:T(8,128)} pad(f32[512,704]{0,1:T(8,128)} %pad_maximum_fusion.4, f32[]{:T(128)} %constant.114.clone.1), padding=0_1_1x0_0_0 | pad | bytes 4325380 | tf_op jit(solution)/shard_map/pad | solution.py:243
  3870.9 57.1 %pad.323 = f32[1024,704]{0,1:T(8,128)} pad(f32[512,704]{0,1:T(8,128)} %add.778, f32[]{:T(128)} %constant.114.clone.1), padding=1_0_1x0_0_0 | pad | bytes 4325380 | tf_op jit(solution)/shard_map/pad | solution.py:243
  4171.8 197.3 %all-reduce.88.cloned.1.call-done = f32[1024,2048]{1,0:T(8,128)} async-done(((f32[1024,2048]{1,0:T(8,128)}), f32[1024,2048]{1,0:T(8,128)}) %all-reduce.88.cloned.1.call-update) | async-done | bytes 8388624 | tf_op jit(solution)/shard_map/psum | solution.py:281
  4408.2 188.9 %reduce-scatter.5.cloned.1.call-done = f32[256,4608]{0,1:T(8,128)} async-done(((f32[2048,4608]{0,1:T(8,128)}), f32[256,4608]{0,1:T(8,128)}) %reduce-scatter.5.cloned.1.call-update) | async-done | bytes 4718608 | tf_op jit(solution)/shard_map/reduce_scatter | solution.py:219
  4607.8 236.8 %all-reduce.90.cloned.1.call-done = (f32[2048,704]{0,1:T(8,128)}, f32[2048,704]{0,1:T(8,128)}, f32[4,176,176]{2,1,0:T(8,128)}, f32[4,176,176]{2,1,0:T(8,128)}, f32[704,2048]{1,0:T(8,128)}) async-done(((f32[2048,704]{0,1:T(8,128)}, f32[2048,704]{0,1:T(8,128)}, f32[4,176,176]{2,1,0:T(8,128)}, f32[4,176,176]{2,1,0:T(8,128)}, f32[704,2048]{1,0:T(8,128)}), (f32[2048,704]{0,1:T(8,128)}, f32[2048,704]{0,1:T(8,128)}, ...) | async-done | bytes 18292752 | tf_op jit(solution)/shard_map/psum | solution.py:299
  (750 shorter events, 1804.3 us)
Async XLA Ops:
  7.2 1545.7 %copy-start = (bf16[2048,704]{0,1:T(8,128)(2,1)S(1)}, bf16[2048,704]{0,1:T(8,128)(2,1)}, u32[]{:S(2)}) copy-start(bf16[2048,704]{0,1:T(8,128)(2,1)} %param.26) | copy-start | bytes 8650756
  7.2 89.8 %copy-start.118 = (f32[2048]{0:T(1024)S(1)}, f32[2048]{0:T(1024)}, u32[]{:S(2)}) copy-start(f32[2048]{0:T(1024)} %param.24) | copy-start | bytes 24580
  7.2 85.9 %all-gather.11.cloned.1.call-start = ((), (), s32[]{:S(2)}) async-start(), calls=%async_computation.2 | async-start | bytes 5242880 | tf_op jit(solution)/shard_map/all_gather | solution.py:120
  8.0 2122.7 %all-gather.19.cloned.1.call-start = ((), (), s32[]{:S(2)}) async-start(), calls=%async_computation.10 | async-start | bytes 41943040 | tf_op jit(solution)/shard_map/all_gather | solution.py:13
  8.8 10.2 collective-permute-start
  11.7 5.4 collective-permute-start.3
  13.1 91.1 %copy-start.126 = (s32[1024]{0:T(1024)}, s32[1024]{0:T(1024)S(1)}, u32[]{:S(2)}) copy-start(s32[1024]{0:T(1024)S(1)} %iota_add_fusion.2) | copy-start | bytes 12292
  13.1 130.5 %copy-start.95 = (s32[1024]{0:T(1024)}, s32[1024]{0:T(1024)S(1)}, u32[]{:S(2)}) copy-start(s32[1024]{0:T(1024)S(1)} %iota_add_fusion.1) | copy-start | bytes 12292
  13.1 100.8 %copy-start.124 = (s32[1024]{0:T(1024)}, s32[1024]{0:T(1024)S(1)}, u32[]{:S(2)}) copy-start(s32[1024]{0:T(1024)S(1)} %iota_add_fusion.4) | copy-start | bytes 12292
  13.1 133.1 %copy-start.97 = (s32[1024]{0:T(1024)}, s32[1024]{0:T(1024)S(1)}, u32[]{:S(2)}) copy-start(s32[1024]{0:T(1024)S(1)} %iota_add_fusion.3) | copy-start | bytes 12292
  13.1 135.7 %copy-start.93 = (s32[1024]{0:T(1024)}, s32[1024]{0:T(1024)S(1)}, u32[]{:S(2)}) copy-start(s32[1024]{0:T(1024)S(1)} %iota_add_fusion.5) | copy-start | bytes 12292
  13.2 110.7 %copy-start.128 = (s32[1024]{0:T(1024)}, s32[1024]{0:T(1024)S(1)}, u32[]{:S(2)}) copy-start(s32[1024]{0:T(1024)S(1)} %iota_add_fusion) | copy-start | bytes 12292
  14.1 137.6 %copy-start.85 = (f32[704]{0:T(1024)}, f32[704]{0:T(1024)S(1)}, u32[]{:S(2)}) copy-start(f32[704]{0:T(1024)S(1)} %get-tuple-element.233) | copy-start | bytes 8452
  14.1 137.6 %copy-start.87 = (f32[704]{0:T(1024)}, f32[704]{0:T(1024)S(1)}, u32[]{:S(2)}) copy-start(f32[704]{0:T(1024)S(1)} %get-tuple-element.234) | copy-start | bytes 8452
  14.1 137.6 %copy-start.89 = (f32[704]{0:T(1024)}, f32[704]{0:T(1024)S(1)}, u32[]{:S(2)}) copy-start(f32[704]{0:T(1024)S(1)} %get-tuple-element.236) | copy-start | bytes 8452
  14.1 137.6 %copy-start.91 = (f32[704]{0:T(1024)}, f32[704]{0:T(1024)S(1)}, u32[]{:S(2)}) copy-start(f32[704]{0:T(1024)S(1)} %get-tuple-element.235) | copy-start | bytes 8452
  15.4 250.3 %copy-start.82 = (f32[704]{0:T(1024)}, f32[704]{0:T(1024)S(1)}, u32[]{:S(2)}) copy-start(f32[704]{0:T(1024)S(1)} %get-tuple-element.390) | copy-start | bytes 8452
  19.0 129.9 %copy-start.99 = (f32[1024]{0:T(1024)}, f32[1024]{0:T(1024)S(1)}, u32[]{:S(2)}) copy-start(f32[1024]{0:T(1024)S(1)} %get-tuple-element.388) | copy-start | bytes 12292
  19.1 124.5 %copy-start.103 = (f32[1024]{0:T(1024)}, f32[1024]{0:T(1024)S(1)}, u32[]{:S(2)}) copy-start(f32[1024]{0:T(1024)S(1)} %get-tuple-element.386) | copy-start | bytes 12292
  19.1 127.1 %copy-start.101 = (f32[1024]{0:T(1024)}, f32[1024]{0:T(1024)S(1)}, u32[]{:S(2)}) copy-start(f32[1024]{0:T(1024)S(1)} %get-tuple-element.285) | copy-start | bytes 12292
  19.1 132.6 %copy-start.105 = (f32[1024]{0:T(1024)}, f32[1024]{0:T(1024)S(1)}, u32[]{:S(2)}) copy-start(f32[1024]{0:T(1024)S(1)} %get-tuple-element.385) | copy-start | bytes 12292
  19.1 246.6 %copy-start.113 = (pred[1024]{0:T(1024)(128)(4,1)}, pred[1024]{0:T(1024)(128)(4,1)S(1)}, u32[]{:S(2)}) copy-start(pred[1024]{0:T(1024)(128)(4,1)S(1)} %get-tuple-element.284) | copy-start | bytes 3076
  97.0 1455.9 %copy-start.110 = (f32[1024]{0:T(1024)}, f32[1024]{0:T(1024)S(1)}, u32[]{:S(2)}) copy-start(f32[1024]{0:T(1024)S(1)} %fusion.172) | copy-start | bytes 12292
  102.2 41.3 collective-permute-start.1
  620.0 56.9 %copy-start.28 = (f32[128,704]{0,1:T(8,128)}, f32[128,704]{0,1:T(8,128)S(1)}, u32[]{:S(2)}) copy-start(f32[128,704]{0,1:T(8,128)S(1)} %get-tuple-element.384) | copy-start | bytes 1081348
  701.3 23.2 copy-start.35
  768.6 15.5 copy-start.32
  1061.5 42.6 copy-start.29
  1117.0 30.0 copy-start.70
  1231.2 85.8 %copy-start.66 = (f32[1,704]{0,1:T(8,128)S(1)}, f32[1,704]{0,1:T(8,128)}, u32[]{:S(2)}) copy-start(f32[1,704]{0,1:T(8,128)} %slice.880) | copy-start | bytes 8452
  1414.5 67.8 %copy-start.63 = (f32[1,704]{0,1:T(8,128)S(1)}, f32[1,704]{0,1:T(8,128)}, u32[]{:S(2)}) copy-start(f32[1,704]{0,1:T(8,128)} %slice.879) | copy-start | bytes 8452
  1571.0 605.3 %all-gather.13.cloned.1.call-start = ((), (), s32[]{:S(2)}) async-start(), calls=%async_computation.3 | async-start | bytes 7077888 | tf_op jit(solution)/shard_map/all_gather | solution.py:190
  1571.7 651.8 %all-gather.15.cloned.1.call-start = ((), (), s32[]{:S(2)}) async-start(), calls=%async_computation.4 | async-start | bytes 7077888 | tf_op jit(solution)/shard_map/all_gather | solution.py:191
  1572.3 699.7 %all-gather.17.cloned.1.call-start = ((), (), s32[]{:S(2)}) async-start(), calls=%async_computation.5 | async-start | bytes 7077888 | tf_op jit(solution)/shard_map/all_gather | solution.py:200
  1572.9 1029.5 %all-reduce.86.cloned.1.call-start = ((), (), s32[]{:S(2)}) async-start(), calls=%async_computation.7 | async-start | bytes 16777216 | tf_op jit(solution)/shard_map/psum | solution.py:214
  2311.4 1856.8 %reduce-scatter.3.cloned.1.call-start = ((), (), s32[]{:S(2)}) async-start(), calls=%async_computation.6 | async-start | bytes 10485760 | tf_op jit(solution)/shard_map/reduce_scatter | solution.py:203
  2528.3 1840.9 %all-reduce.88.cloned.1.call-start = ((), (), s32[]{:S(2)}) async-start(), calls=%async_computation.8 | async-start | bytes 16777216 | tf_op jit(solution)/shard_map/psum | solution.py:281
  3497.3 45.6 copy-start.68
  3565.0 58.7 %copy-start.64 = (f32[1,704]{0,1:T(8,128)S(1)}, f32[1,704]{0,1:T(8,128)}, u32[]{:S(2)}) copy-start(f32[1,704]{0,1:T(8,128)} %slice.944) | copy-start | bytes 8452
  3784.8 25.8 copy-start.61
  3933.2 46.8 copy-start.83
  3933.2 46.8 copy-start.114
  4025.6 42.3 collective-permute-start.2
  4079.2 518.0 %reduce-scatter.5.cloned.1.call-start = ((), (), s32[]{:S(2)}) async-start(), calls=%async_computation.9 | async-start | bytes 42467328 | tf_op jit(solution)/shard_map/reduce_scatter | solution.py:219
  4135.6 709.0 %all-reduce.90.cloned.1.call-start = ((), (), s32[]{:S(2)}) async-start(), calls=%async_computation.11 | async-start | bytes 37486592 | tf_op jit(solution)/shard_map/psum | solution.py:299
  4171.8 205.4 %copy-start.112 = (f32[2048]{0:T(1024)S(1)}, f32[2048]{0:T(1024)}, u32[]{:S(2)}) copy-start(f32[2048]{0:T(1024)} %get-tuple-element.220) | copy-start | bytes 24580
  4171.8 205.4 %copy-start.115 = (f32[704]{0:T(1024)S(1)}, f32[704]{0:T(1024)}, u32[]{:S(2)}) copy-start(f32[704]{0:T(1024)} %get-tuple-element.270) | copy-start | bytes 8452
  4171.8 230.9 %copy-start.108 = (f32[1024]{0:T(1024)S(1)}, f32[1024]{0:T(1024)}, u32[]{:S(2)}) copy-start(f32[1024]{0:T(1024)} %copy-done.107) | copy-start | bytes 12292
  (111 other events, 626.2 us)
Sparse Core Ops, SparseCore 0:
  9.6 83.4 all-gather.10
  1571.1 559.4 all-gather.18
  2132.5 43.6 all-gather.12
  2178.0 45.5 all-gather.14
  2225.3 46.6 all-gather.16
  2311.5 290.8 all-reduce.85
  2604.8 143.4 reduce-scatter.2
  4079.3 289.7 all-reduce.87
  4372.7 224.3 reduce-scatter.4
  4603.5 241.0 all-reduce.89
